TPU v7x, 32 devices: a whole 2x2x4 slice. The times are simulated.
32 devices in a mesh: row: 4 (over z), col: 8 (over y, x, core).
Axes of the slice: x: 2, y: 2, z: 4, core: 2. Of those that a mesh axis runs over, the one named last changes fastest.
Arguments:
- dec_src: float32 [2304, 8192], P('col', 'row'), may hold values from -6 to 6
- enc_tgt: float32 [2304, 16384], P('row', 'col'), may hold values from -0.125 to 0.125
- src_coacts: float32 [512, 8192], P('col', 'row'), may hold values from -6 to 6
- tgt_coacts: float32 [512, 16384], P('row', 'col'), may hold values from -6 to 6
- eval_src: float32 [512, 8192], P('col', 'row'), may hold values from -6 to 6
- enc_bias: float32 [16384], P('col'), may hold values from -0.5 to 0.5
- dec_tgt: float32 [2304, 16384], P('row', 'col'), may hold values from -0.046875 to 0.046875
- tile_mask: int32 [128, 256], P('row', 'col'), may hold values from 0 to 1, as said below
Outputs:
- recon: float32 [512, 2304], P('col', 'row')
Inputs may be any that keep to these rules, and one draw needn't show every extreme that they name: `tile_mask`: 1 keeps a tile, 0 prunes it; the share of kept tiles differs between regions of the grid.
All inputs are finite; a program needn't handle non-finite values.
Results may differ from a plain program's by a relative error of at most 0.0003.
Values sent between devices are 32-bit elements; how exact they have to be, the bound alone decides.
A program may use at most 192 MiB of HBM per device.

v0:
```python
import jax
import jax.numpy as jnp
from jax import lax
from jax.sharding import PartitionSpec as P

S = 8192
TILE = 64
PRECISE = lax.Precision.HIGHEST


def contract_first(left, right):
    return lax.dot_general(
        left, right, (((0,), (0,)), ((), ())), precision=PRECISE, preferred_element_type=jnp.float32
    )


def local(dec_src, enc_tgt, src_coacts, tgt_coacts, eval_src, enc_bias, dec_tgt, tile_mask):
    src_count = dec_src.shape[1]
    tgt_count = enc_tgt.shape[1]
    enc_full = lax.all_gather(enc_tgt, "row", axis=0, tiled=True)
    src_full, eval_full = (
        lax.all_gather(src_coacts, "col", axis=0, tiled=True),
        lax.all_gather(eval_src, "col", axis=0, tiled=True),
    )
    virtual = contract_first(lax.all_gather(dec_src, "col", axis=0, tiled=True), enc_full)
    coact = contract_first(src_full, lax.all_gather(tgt_coacts, "row", axis=0, tiled=True))
    coact = coact * (1.0 / jnp.sqrt(jnp.float32(src_full.shape[0])))
    tile_rows, tile_cols = tile_mask.shape
    mask_float = tile_mask.astype(jnp.float32)
    weighted = (
        (virtual * coact).reshape(tile_rows, TILE, tile_cols, TILE) * mask_float[:, None, :, None]
    ).reshape(src_count, tgt_count)
    partial_pre = jnp.dot(
        eval_full, weighted, precision=PRECISE, preferred_element_type=jnp.float32
    )
    scale = 1.0 / jnp.sqrt(jnp.float32(S))
    pre_acts = lax.psum(partial_pre, "row")
    hidden = jnp.maximum(pre_acts * scale + enc_bias[None, :], 0.0)
    recon_part = lax.dot_general(
        hidden,
        dec_tgt,
        (((1,), (1,)), ((), ())),
        precision=PRECISE,
        preferred_element_type=jnp.float32,
    )
    return lax.psum_scatter(recon_part, "col", scatter_dimension=0, tiled=True)


def solution(mesh):
    return jax.shard_map(
        local,
        mesh=mesh,
        in_specs=(
            P("col", "row"),
            P("row", "col"),
            P("col", "row"),
            P("row", "col"),
            P("col", "row"),
            P("col"),
            P("row", "col"),
            P("row", "col"),
        ),
        out_specs=P("col", "row"),
        check_vma=False,
    )
```

profile of v0, /device:TPU:0, one launch (start us, length us, event | category | flops | bytes accessed | tf_op | source)
XLA Modules:
  0.0 963.4 jit_solution(13110801990855593298)
XLA Ops:
  6.5 0.0 copy-start
  6.5 0.0 all-gather.12.cloned.1.call-start
  6.5 0.7 all-gather.12.cloned.1.call-update
  7.3 0.0 all-gather.10.cloned.1.call-start
  7.3 0.7 all-gather.10.cloned.1.call-update
  8.0 0.0 all-gather.8.cloned.1.call-start
  8.1 0.7 all-gather.8.cloned.1.call-update
  8.7 0.0 all-gather.6.cloned.1.call-start
  8.8 0.5 all-gather.6.cloned.1.call-update
  9.3 0.0 all-gather.14.cloned.1.call-start
  9.4 0.5 all-gather.14.cloned.1.call-update
  9.9 0.0 all-reduce.2.cloned.1.call-start
  10.0 0.0 copy-done
  10.0 11.9 %mul.29 = f32[32,64,32,64]{3,2,1,0:T(8,128)} broadcast(f32[32,32]{1,0:T(8,128)S(1)} %convert_element_type.3), dimensions={0,2} | broadcast | bytes 16781312 | tf_op jit(solution)/shard_map/mul | solution.py:31
  21.9 29.0 %mul.30 = f32[2048,2048]{1,0:T(8,128)} reshape(f32[32,64,32,64]{3,2,1,0:T(8,128)} %mul.29) | data formatting | bytes 33554432 | tf_op jit(solution)/shard_map/mul | solution.py:31
  50.9 41.5 %all-gather.12.cloned.1.call-done = f32[512,2048]{1,0:T(8,128)} async-done(((f32[128,2048]{1,0:T(8,128)}), f32[512,2048]{1,0:T(8,128)}) %all-gather.12.cloned.1.call-update) | async-done | bytes 4194320 | tf_op jit(solution)/shard_map/all_gather | solution.py:26
  92.4 37.0 %all-gather.10.cloned.1.call-done = f32[512,2048]{1,0:T(8,128)} async-done(((f32[64,2048]{1,0:T(8,128)}), f32[512,2048]{1,0:T(8,128)}) %all-gather.10.cloned.1.call-update) | async-done | bytes 4194320 | tf_op jit(solution)/shard_map/all_gather | solution.py:22
  129.4 31.4 %fusion.19 = f32[2048,2048]{1,0:T(8,128)} fusion(f32[512,2048]{1,0:T(8,128)} %all-gather.10.cloned.1.call-done, f32[512,2048]{1,0:T(8,128)} %all-gather.12.cloned.1.call-done), kind=kOutput, calls=%fused_computation.17 | convolution fusion | flops 25769803776 | bytes 25165824 | tf_op jit(solution)/shard_map/dot_general | solution.py:12
  160.8 292.8 %all-gather.8.cloned.1.call-done = f32[2304,2048]{1,0:T(8,128)} async-done(((f32[576,2048]{1,0:T(8,128)}), f32[2304,2048]{1,0:T(8,128)}) %all-gather.8.cloned.1.call-update) | async-done | bytes 18874384 | tf_op jit(solution)/shard_map/all_gather | solution.py:20
  453.6 99.2 %all-gather.6.cloned.1.call-done = f32[2304,2048]{1,0:T(8,128)} async-done(((f32[288,2048]{1,0:T(8,128)}), f32[2304,2048]{1,0:T(8,128)}) %all-gather.6.cloned.1.call-update) | async-done | bytes 18874384 | tf_op jit(solution)/shard_map/all_gather | solution.py:25
  552.8 125.5 %fusion.18 = f32[2048,2048]{1,0:T(8,128)} fusion(f32[2304,2048]{1,0:T(8,128)} %all-gather.6.cloned.1.call-done, f32[2304,2048]{1,0:T(8,128)} %all-gather.8.cloned.1.call-done), kind=kOutput, calls=%fused_computation.16 | convolution fusion | flops 115964116992 | bytes 54525952 | tf_op jit(solution)/shard_map/dot_general | solution.py:12
  678.3 0.0 copy-start.1
  678.3 0.0 all-gather.14.cloned.1.call-done
  678.4 62.9 %fusion.9 = f32[512,2048]{0,1:T(8,128)} fusion(f32[512,2048]{1,0:T(8,128)} %all-gather.14.cloned.1.call-done, f32[2048,2048]{1,0:T(8,128)} %mul.30, f32[2048,2048]{1,0:T(8,128)} %fusion.18, f32[2048,2048]{1,0:T(8,128)} %fusion.19), kind=kOutput, calls=%fused_computation.9 | convolution fusion | flops 25782386688 | bytes 58720256 | tf_op jit(solution)/shard_map/dot_general | solution.py:33
  741.2 0.0 all-reduce.2.cloned.1.call-update
  741.3 0.0 reduce-scatter.2.cloned.1.call-start
  741.3 155.1 %all-reduce.2.cloned.1.call-done = f32[512,2048]{0,1:T(8,128)} async-done(((f32[512,2048]{0,1:T(8,128)}), f32[512,2048]{0,1:T(8,128)}) %all-reduce.2.cloned.1.call-update) | async-done | bytes 4194320 | tf_op jit(solution)/shard_map/psum | solution.py:37
  896.4 0.0 copy-done.1
  896.4 23.6 %fusion.5 = f32[512,576]{1,0:T(8,128)} fusion(f32[576,2048]{1,0:T(8,128)} %param.14, f32[512,2048]{0,1:T(8,128)} %all-reduce.2.cloned.1.call-done, f32[2048]{0:T(1024)S(1)} %copy-done.1), kind=kOutput, calls=%fused_computation.5 | convolution fusion | flops 7250903040 | bytes 10100736 | tf_op jit(solution)/shard_map/dot_general | solution.py:39
  920.1 0.0 reduce-scatter.2.cloned.1.call-update
  920.1 36.3 %reduce-scatter.2.cloned.1.call-done = f32[64,576]{1,0:T(8,128)} async-done(((f32[512,576]{1,0:T(8,128)}), f32[64,576]{1,0:T(8,128)}) %reduce-scatter.2.cloned.1.call-update) | async-done | bytes 147472 | tf_op jit(solution)/shard_map/reduce_scatter | solution.py:46
  (1 shorter events, 0.0 us)
Async XLA Ops:
  6.5 3.4 copy-start
  6.5 85.9 %all-gather.12.cloned.1.call-start = ((), (), s32[]{:S(2)}) async-start(), calls=%async_computation.4 | async-start | bytes 5242880 | tf_op jit(solution)/shard_map/all_gather | solution.py:26
  7.3 122.1 %all-gather.10.cloned.1.call-start = ((), (), s32[]{:S(2)}) async-start(), calls=%async_computation.3 | async-start | bytes 4718592 | tf_op jit(solution)/shard_map/all_gather | solution.py:22
  8.0 445.6 %all-gather.8.cloned.1.call-start = ((), (), s32[]{:S(2)}) async-start(), calls=%async_computation.2 | async-start | bytes 23592960 | tf_op jit(solution)/shard_map/all_gather | solution.py:20
  8.7 544.0 %all-gather.6.cloned.1.call-start = ((), (), s32[]{:S(2)}) async-start(), calls=%async_computation.1 | async-start | bytes 21233664 | tf_op jit(solution)/shard_map/all_gather | solution.py:25
  9.3 669.0 %all-gather.14.cloned.1.call-start = ((), (), s32[]{:S(2)}) async-start(), calls=%async_computation.5 | async-start | bytes 4718592 | tf_op jit(solution)/shard_map/all_gather | solution.py:23
  9.9 886.5 %all-reduce.2.cloned.1.call-start = ((), (), s32[]{:S(2)}) async-start(), calls=%async_computation.6 | async-start | bytes 8388608 | tf_op jit(solution)/shard_map/psum | solution.py:37
  678.3 218.1 %copy-start.1 = (f32[2048]{0:T(1024)S(1)}, f32[2048]{0:T(1024)}, u32[]{:S(2)}) copy-start(f32[2048]{0:T(1024)} %param.13) | copy-start | bytes 24580
  741.3 215.1 %reduce-scatter.2.cloned.1.call-start = ((), (), s32[]{:S(2)}) async-start(), calls=%async_computation.7 | async-start | bytes 1474560 | tf_op jit(solution)/shard_map/reduce_scatter | solution.py:46
Sparse Core Ops, SparseCore 0:
  8.9 83.4 all-gather.11
  94.3 35.0 all-gather.9
  131.0 322.5 all-gather.7
  455.3 97.4 all-gather.5
  554.5 36.5 all-gather.13
  741.4 154.9 all-reduce.1
  920.2 36.1 reduce-scatter.1
where the time goes:
time: 970 us; the launch traced here: 963 us
  waiting for transfers between devices  665 us (69%)
  matrix products  243 us (25%)
  local copies, waits for them, and re-layouts  40.9 us (4%)
  between operations  13.7 us (1%)
    all_gather x1, waiting for transfers between devices, local(): enc_full = lax.all_gather(enc_tgt, 'row', axis=0, tiled=True)  293 us
    dot_general x2, matrix products, contract_first(): lax.dot_general(left, right, (((0,), (0,)), ((), ())), precision=PRECISE,...  157 us
    psum x1, waiting for transfers between devices, local(): pre_acts = lax.psum(partial_pre, 'row')  155 us
    all_gather x1, waiting for transfers between devices, local(): lax.all_gather(dec_src, 'col', axis=0, tiled=True)  99.2 us
    dot_general x1, matrix products, local(): jnp.dot(eval_full, weighted, precision=PRECISE, preferred_element_type=jn...  62.9 us
    all_gather x1, waiting for transfers between devices, local(): lax.all_gather(tgt_coacts, 'row', axis=0, tiled=True)  41.5 us
    mul x2, local copies, waits for them, and re-layouts, local(): (virtual * coact).reshape(tile_rows, TILE, tile_cols, TILE)  40.9 us
    all_gather x1, waiting for transfers between devices, local(): lax.all_gather(src_coacts, 'col', axis=0, tiled=True)  37 us
  transfers between devices with their start and end apart: 7, of which 6 were waited for; matrix products, arithmetic and copies ran while one was open for 21% of the time, Pallas kernels for 0%

commit v1 on v0

--- a/solution.py
+++ b/solution.py
@@ -17,7 +17,12 @@
 def local(dec_src, enc_tgt, src_coacts, tgt_coacts, eval_src, enc_bias, dec_tgt, tile_mask):
     src_count = dec_src.shape[1]
     tgt_count = enc_tgt.shape[1]
-    enc_full = lax.all_gather(enc_tgt, "row", axis=0, tiled=True)
+    ring = [enc_tgt]
+    for hop in range(3):
+        ring.append(lax.ppermute(ring[-1], "row", [(dev, (dev + 1) % 4) for dev in range(4)]))
+    enc_full = jnp.roll(
+        jnp.concatenate(ring[::-1], axis=0), (lax.axis_index("row") + 1) * ring[0].shape[0], axis=0
+    )
     src_full, eval_full = (
         lax.all_gather(src_coacts, "col", axis=0, tiled=True),
         lax.all_gather(eval_src, "col", axis=0, tiled=True),

time: 970 us -> 822 us (0.85)
  waiting for transfers between devices: 665 us -> 500 us
  local copies, waits for them, and re-layouts: 40.9 us -> 76 us
  matrix products: 243 us -> 220 us
    ppermute x0 -> x3, waiting for transfers between devices: none -> 308 us  [local(): lax.ppermute(ring[-1], 'row', [(dev, (dev + 1) % 4) for dev in range(4)])]
    all_gather x1 -> x0, waiting for transfers between devices: 293 us -> none  [local(): enc_full = lax.all_gather(enc_tgt, 'row', axis=0, tiled=True)]
    all_gather x1, waiting for transfers between devices: 99.2 us -> 0.01 us  [local(): lax.all_gather(dec_src, 'col', axis=0, tiled=True)]
    all_gather x1, waiting for transfers between devices: 41.5 us -> 0.01 us  [local(): lax.all_gather(tgt_coacts, 'row', axis=0, tiled=True)]
    all_gather x1, waiting for transfers between devices: 37 us -> 0.01 us  [local(): lax.all_gather(src_coacts, 'col', axis=0, tiled=True)]
    unnamed x4 -> x19, local copies, waits for them, and re-layouts: 0.01 us -> 33.3 us
    dot_general x1, matrix products: 62.9 us -> 37.9 us  [local(): jnp.dot(eval_full, weighted, precision=PRECISE, preferred_element_type=jn...]
  transfers between devices with their start and end apart: 7 -> 9, of which waited for: 6 -> 5; matrix products, arithmetic and copies ran while one was open for 21% -> 29% of each run, Pallas kernels for 0% -> 0%
where the time goes in v1:
time: 822 us; the launch traced here: 813 us
  waiting for transfers between devices  500 us (61%)
  matrix products  220 us (27%)
  local copies, waits for them, and re-layouts  76 us (9%)
  between operations  13.9 us (2%)
    ppermute x3, waiting for transfers between devices, local(): lax.ppermute(ring[-1], 'row', [(dev, (dev + 1) % 4) for dev in range(4)])  308 us
    dot_general x2, matrix products, contract_first(): lax.dot_general(left, right, (((0,), (0,)), ((), ())), precision=PRECISE,...  158 us
    psum x1, waiting for transfers between devices, local(): pre_acts = lax.psum(partial_pre, 'row')  153 us
    mul x2, local copies, waits for them, and re-layouts, local(): (virtual * coact).reshape(tile_rows, TILE, tile_cols, TILE)  39.8 us
    dot_general x1, matrix products, local(): jnp.dot(eval_full, weighted, precision=PRECISE, preferred_element_type=jn...  37.9 us
    reduce_scatter x1, waiting for transfers between devices, local(): return lax.psum_scatter(recon_part, 'col', scatter_dimension=0, tiled=True)  36.3 us
    unnamed x19, local copies, waits for them, and re-layouts  33.3 us
    dot_general x1, matrix products, local(): lax.dot_general(hidden, dec_tgt, (((1,), (1,)), ((), ())), precision=PREC...  23.6 us
  transfers between devices with their start and end apart: 9, of which 5 were waited for; matrix products, arithmetic and copies ran while one was open for 29% of the time, Pallas kernels for 0%

profile of v1, /device:TPU:0, one launch (start us, length us, event | category | flops | bytes accessed | tf_op | source)
XLA Modules:
  0.0 813.2 jit_solution(17789372261125082259)
XLA Ops:
  6.5 0.7 all-gather.9.cloned.1.call-update
  7.3 0.0 all-gather.7.cloned.1.call-start
  7.3 0.7 all-gather.7.cloned.1.call-update
  8.0 0.0 all-gather.5.cloned.1.call-start
  8.1 0.7 all-gather.5.cloned.1.call-update
  8.7 0.0 all-gather.11.cloned.1.call-start
  8.8 3.1 collective-permute-start
  11.9 171.5 %collective-permute-done = f32[576,2048]{1,0:T(8,128)S(1)} collective-permute-done((f32[576,2048]{1,0:T(8,128)}, f32[576,2048]{1,0:T(8,128)S(1)}, u32[]{:S(2)}, u32[]{:S(2)}) %collective-permute-start) | collective-permute-done | bytes 4718624 | tf_op jit(solution)/shard_map/ppermute | solution.py:22
  183.4 2.1 copy-done
  185.6 104.9 %collective-permute-done.1 = f32[576,2048]{1,0:T(8,128)} collective-permute-done((f32[576,2048]{1,0:T(8,128)S(1)}, f32[576,2048]{1,0:T(8,128)}, u32[]{:S(2)}, u32[]{:S(2)}) %collective-permute-start.1) | collective-permute-done | bytes 4718624 | tf_op jit(solution)/shard_map/ppermute | solution.py:22
  290.5 0.0 all-reduce.2.cloned.1.call-start
  290.6 0.7 convert_element_type.3
  291.3 0.1 copy.9
  291.4 11.4 %mul.33 = f32[32,64,32,64]{1,0,3,2:T(8,128)} broadcast(f32[32,32]{0,1:T(8,128)S(1)} %copy.9), dimensions={0,2} | broadcast | bytes 16781312 | tf_op jit(solution)/shard_map/mul | solution.py:36
  302.7 28.4 %mul.34 = f32[2048,2048]{0,1:T(8,128)} reshape(f32[32,64,32,64]{1,0,3,2:T(8,128)} %mul.33) | data formatting | bytes 33554432 | tf_op jit(solution)/shard_map/mul | solution.py:36
  331.1 31.7 %fusion.21 = f32[2048,2048]{0,1:T(8,128)} fusion(f32[512,2048]{1,0:T(8,128)} %all-gather.7.cloned.1.call-done, f32[512,2048]{1,0:T(8,128)} %all-gather.9.cloned.1.call-done), kind=kOutput, calls=%fused_computation.27 | convolution fusion | flops 25769803776 | bytes 25165824 | tf_op jit(solution)/shard_map/dot_general | solution.py:12
  362.9 31.8 %collective-permute-done.2 = f32[576,2048]{1,0:T(8,128)} collective-permute-done((f32[576,2048]{1,0:T(8,128)}, f32[576,2048]{1,0:T(8,128)}, u32[]{:S(2)}, u32[]{:S(2)}) %collective-permute-start.2) | collective-permute-done | bytes 4718624 | tf_op jit(solution)/shard_map/ppermute | solution.py:22
  394.7 5.1 constant_dynamic-update-slice_fusion.7
  399.7 5.2 constant_dynamic-update-slice_fusion.6
  404.9 5.3 constant_dynamic-update-slice_fusion.5
  410.2 2.7 constant_dynamic-update-slice_fusion.4
  412.9 5.2 constant_dynamic-update-slice_fusion.3
  418.1 5.1 constant_dynamic-update-slice_fusion.2
  423.2 2.7 constant_dynamic-update-slice_fusion.1
  425.8 2.8 constant_dynamic-update-slice_fusion
  428.7 126.5 %fusion = f32[2048,2048]{1,0:T(8,128)} fusion(f32[2304,2048]{1,0:T(8,128)} %all-gather.5.cloned.1.call-done, f32[4608,2048]{1,0:T(8,128)} %constant_dynamic-update-slice_fusion, s32[]{:T(128)S(6)} %select_n.14), kind=kOutput, calls=%fused_computation | convolution fusion | flops 115964116992 | bytes 54525956 | tf_op jit(solution)/shard_map/dot_general | solution.py:12
  555.2 0.0 all-gather.11.cloned.1.call-done
  555.2 37.9 %fusion.11 = f32[512,2048]{0,1:T(8,128)} fusion(f32[512,2048]{1,0:T(8,128)} %all-gather.11.cloned.1.call-done, f32[2048,2048]{0,1:T(8,128)} %mul.34, f32[2048,2048]{1,0:T(8,128)} %fusion, f32[2048,2048]{0,1:T(8,128)} %fusion.21), kind=kOutput, calls=%fused_computation.11 | convolution fusion | flops 25782386688 | bytes 58720256 | tf_op jit(solution)/shard_map/dot_general | solution.py:38
  593.1 0.0 reduce-scatter.2.cloned.1.call-start
  593.2 152.9 %all-reduce.2.cloned.1.call-done = f32[512,2048]{0,1:T(8,128)} async-done(((f32[512,2048]{0,1:T(8,128)}), f32[512,2048]{0,1:T(8,128)}) %all-reduce.2.cloned.1.call-update) | async-done | bytes 4194320 | tf_op jit(solution)/shard_map/psum | solution.py:42
  746.0 23.6 %fusion.7 = f32[512,576]{1,0:T(8,128)} fusion(f32[576,2048]{1,0:T(8,128)} %param.14, f32[512,2048]{0,1:T(8,128)} %all-reduce.2.cloned.1.call-done, f32[2048]{0:T(1024)S(1)} %copy-done.1), kind=kOutput, calls=%fused_computation.7 | convolution fusion | flops 7250903040 | bytes 10100736 | tf_op jit(solution)/shard_map/dot_general | solution.py:44
  769.7 36.3 %reduce-scatter.2.cloned.1.call-done = f32[64,576]{1,0:T(8,128)} async-done(((f32[512,576]{1,0:T(8,128)}), f32[64,576]{1,0:T(8,128)}) %reduce-scatter.2.cloned.1.call-update) | async-done | bytes 147472 | tf_op jit(solution)/shard_map/reduce_scatter | solution.py:51
  (22 shorter events, 0.1 us)
Async XLA Ops:
  6.5 324.6 %all-gather.9.cloned.1.call-start = ((), (), s32[]{:S(2)}) async-start(), calls=%async_computation.3 | async-start | bytes 5242880 | tf_op jit(solution)/shard_map/all_gather | solution.py:31
  7.3 323.9 %all-gather.7.cloned.1.call-start = ((), (), s32[]{:S(2)}) async-start(), calls=%async_computation.2 | async-start | bytes 4718592 | tf_op jit(solution)/shard_map/all_gather | solution.py:27
  8.0 420.6 %all-gather.5.cloned.1.call-start = ((), (), s32[]{:S(2)}) async-start(), calls=%async_computation.1 | async-start | bytes 21233664 | tf_op jit(solution)/shard_map/all_gather | solution.py:30
  8.7 546.5 %all-gather.11.cloned.1.call-start = ((), (), s32[]{:S(2)}) async-start(), calls=%async_computation.4 | async-start | bytes 4718592 | tf_op jit(solution)/shard_map/all_gather | solution.py:28
  8.8 174.6 %collective-permute-start = (f32[576,2048]{1,0:T(8,128)}, f32[576,2048]{1,0:T(8,128)S(1)}, u32[]{:S(2)}, u32[]{:S(2)}) collective-permute-start(f32[576,2048]{1,0:T(8,128)} %param.9), channel_id=1, source_target_pairs={{0,8},{8,16},{16,24},{24,0},{1,9},{9,17},{17,25},{25,1},{2,10},{10... | collective-permute-start | bytes 14155784 | tf_op jit(solution)/shard_map/ppermute | solution.py:22
  183.4 2.1 copy-start
  185.6 104.9 %collective-permute-start.1 = (f32[576,2048]{1,0:T(8,128)S(1)}, f32[576,2048]{1,0:T(8,128)}, u32[]{:S(2)}, u32[]{:S(2)}) collective-permute-start(f32[576,2048]{1,0:T(8,128)S(1)} %collective-permute-done), channel_id=1, source_target_pairs={{0,8},{8,16},{16,24},{24,0},{1,9},{9,17},{17,25},{25,1},{2,10},{10... | collective-permute-start | bytes 14155784 | tf_op jit(solution)/shard_map/ppermute | solution.py:22
  290.5 104.2 %collective-permute-start.2 = (f32[576,2048]{1,0:T(8,128)}, f32[576,2048]{1,0:T(8,128)}, u32[]{:S(2)}, u32[]{:S(2)}) collective-permute-start(f32[576,2048]{1,0:T(8,128)} %collective-permute-done.1), channel_id=1, source_target_pairs={{0,8},{8,16},{16,24},{24,0},{1,9},{9,17},{17,25},{25,1},{2,10},{10... | collective-permute-start | bytes 14155784 | tf_op jit(solution)/shard_map/ppermute | solution.py:22
  290.5 455.6 %all-reduce.2.cloned.1.call-start = ((), (), s32[]{:S(2)}) async-start(), calls=%async_computation.5 | async-start | bytes 8388608 | tf_op jit(solution)/shard_map/psum | solution.py:42
  362.9 47.3 %slice-start = ((s8[4718592]{0:T(1024)(128)(4,1)}), s8[4194304]{0:T(1024)(128)(4,1)S(1)}, s32[]{:S(2)}) async-start(s8[4718592]{0:T(1024)(128)(4,1)} %bitcast.19), calls=%async_computation.7 | async-start | bytes 8388608
  399.7 10.5 %slice-start.1 = ((s8[4718592]{0:T(1024)(128)(4,1)}), s8[524288]{0:T(1024)(128)(4,1)S(1)}, s32[]{:S(2)}) async-start(s8[4718592]{0:T(1024)(128)(4,1)} %bitcast.19), calls=%async_computation.8 | async-start | bytes 1048576
  404.9 18.3 %slice-start.2 = ((s8[4718592]{0:T(1024)(128)(4,1)}), s8[4194304]{0:T(1024)(128)(4,1)S(1)}, s32[]{:S(2)}) async-start(s8[4718592]{0:T(1024)(128)(4,1)} %bitcast.21), calls=%async_computation.9 | async-start | bytes 8388608
  412.9 10.3 %slice-start.3 = ((s8[4718592]{0:T(1024)(128)(4,1)}), s8[524288]{0:T(1024)(128)(4,1)S(1)}, s32[]{:S(2)}) async-start(s8[4718592]{0:T(1024)(128)(4,1)} %bitcast.21), calls=%async_computation.10 | async-start | bytes 1048576
  555.2 190.9 %copy-start.1 = (f32[2048]{0:T(1024)S(1)}, f32[2048]{0:T(1024)}, u32[]{:S(2)}) copy-start(f32[2048]{0:T(1024)} %param.13) | copy-start | bytes 24580
  593.1 212.9 %reduce-scatter.2.cloned.1.call-start = ((), (), s32[]{:S(2)}) async-start(), calls=%async_computation.6 | async-start | bytes 1474560 | tf_op jit(solution)/shard_map/reduce_scatter | solution.py:51
Sparse Core Ops, SparseCore 0:
  8.9 150.7 all-gather.8
  161.6 34.8 all-gather.6
  198.3 98.5 all-gather.4
  298.7 36.5 all-gather.10
  593.2 152.7 all-reduce.1
  769.8 36.1 reduce-scatter.1
